TPU v7x, 512 devices: a whole 4x4x16 slice. The times are simulated.
512 devices in a mesh: row: 32 (over x, y, core), col: 16 (over z).
Axes of the slice: x: 4, y: 4, z: 16, core: 2. Of those that a mesh axis runs over, the one named last changes fastest.
Arguments:
- diag_blocks: bfloat16 [4096, 128, 128], P(('row', 'col')), may hold values from -0.03 to 3, as said below
- off_blocks: bfloat16 [4096, 6, 128, 128], P(('row', 'col')), may hold values from -0.375 to 0.375
- neighbors: int32 [4096, 6], P(('row', 'col')), may hold values from -1 to 4095, as said below
- levels: int32 [4096], P(('row', 'col')), may hold values from 0 to 1, as said below
Outputs:
- pivot_inverse: bfloat16 [4096, 128, 128], P(('row', 'col'))
- factor_blocks: bfloat16 [4096, 6, 128, 128], P(('row', 'col'))
Inputs may be any that keep to these rules, and one draw needn't show every extreme that they name: `levels`: block row i lies on device number d = i // 8, where d = r * (number of devices along col) + c for the device with index r along row and index c along col. On each device the rows of level 0 come first; a device holds between 2 and 6 rows of level 0, and in every draw some device holds exactly 6 and some exactly 2. `neighbors`: A live slot names a row of the other level. Slot 0 names a row on the device whose row index is one higher, slot 1 one lower, slot 2 on the device whose col index is one higher, slot 3 one lower, slots 4 and 5 on the same device. If row i names row j in slot k, row j names row i in slot (1, 0, 3, 2, 5, 4)[k]. `diag_blocks`: diagonal entries from 1 to 3; off-diagonal entries of either sign, each row's sum of their magnitudes under 0.9 times that row's diagonal entry.
All inputs are finite; a program needn't handle non-finite values.
Results may differ from a plain program's by a relative error of at most 0.0053.
Values may be sent and summed in bfloat16 or wider, within the bound.
A program may use at most 64 MiB of HBM per device.

v0:
```python
import jax
import jax.numpy as jnp
from jax import lax
from jax.sharding import PartitionSpec as P

NS_STEPS = 4


MIRROR = (1, 0, 3, 2, 5, 4)


def padded(value, sides, width):
    for axis, dim in sides:
        size, length = (lax.axis_size(axis), value.shape[dim])
        up = [(i, (i + 1) % size) for i in range(size - 1)]
        down = [(j, i) for i, j in up]
        last = lax.slice_in_dim(value, length - width, length, axis=dim)
        initial = lax.slice_in_dim(value, 0, width, axis=dim)
        before = lax.ppermute(last, axis, up)
        after = lax.ppermute(initial, axis, down)
        value = jnp.concatenate([before, value, after], axis=dim)
    return value


def approx_inverse(matrix):
    magnitude = jnp.abs(matrix)
    column_norm = jnp.max(jnp.sum(magnitude, axis=1), axis=1)
    row_norm = jnp.max(jnp.sum(magnitude, axis=2), axis=1)
    iterate = jnp.swapaxes(matrix, 1, 2) / (column_norm * row_norm)[:, None, None]
    for step_index in range(NS_STEPS):
        product = jnp.einsum("nij,njk->nik", matrix, iterate, precision=lax.Precision.HIGHEST)
        iterate = 2.0 * iterate - jnp.einsum(
            "nij,njk->nik", iterate, product, precision=lax.Precision.HIGHEST
        )
    return iterate


def shards(diag_blocks, off_blocks, neighbors, levels):
    rows_here = diag_blocks.shape[0]
    capacity = 3 * rows_here // 4
    slot_count = off_blocks.shape[1]
    block_size = diag_blocks.shape[1]
    active = neighbors >= 0
    first_inverse = approx_inverse(diag_blocks[:capacity].astype(jnp.float32)).astype(jnp.bfloat16)
    upper_rows = jnp.einsum(
        "nij,nkjl->nkil", first_inverse, off_blocks[:capacity], preferred_element_type=jnp.float32
    )
    upper_rows = jnp.where(active[:capacity, :, None, None], upper_rows, 0.0).astype(jnp.bfloat16)

    def paired(source_blocks, source_inverse, slot_index):
        return jnp.stack((source_blocks[:, slot_index], source_inverse), axis=1)

    packed = jnp.concatenate([upper_rows, first_inverse[:, None]], axis=1)
    extended = padded(packed[None, None], (("row", 0), ("col", 1)), 1)
    sources = [extended[2, 1], extended[0, 1], extended[1, 2], extended[1, 0], packed, packed]
    tables = [
        paired(sources[slot_index], sources[slot_index][:, slot_count], MIRROR[slot_index])
        for slot_index in range(slot_count)
    ]
    table = jnp.stack(tables, axis=0)
    start = rows_here - capacity
    later_named = neighbors[start:]
    later_active = active[start:]
    local_rows = jnp.clip(jnp.where(later_active, later_named % rows_here, 0), 0, capacity - 1)
    picked = table[jnp.arange(slot_count)[None, :], local_rows]
    lower_blocks = jnp.where(
        later_active[:, :, None, None], off_blocks[start:], jnp.zeros((), jnp.bfloat16)
    )
    lower_factor = jnp.einsum(
        "qkij,qkjl->qkil", lower_blocks, picked[:, :, 1], preferred_element_type=jnp.float32
    ).astype(jnp.bfloat16)
    schur = jnp.einsum(
        "qkij,qkjl->qil", lower_blocks, picked[:, :, 0], preferred_element_type=jnp.float32
    )
    second_inverse = approx_inverse(diag_blocks[start:].astype(jnp.float32) - schur).astype(
        jnp.bfloat16
    )
    early = levels == 0
    pivot_first = jnp.concatenate(
        [first_inverse, jnp.zeros((start, block_size, block_size), jnp.bfloat16)], axis=0
    )
    pivot_second = jnp.concatenate(
        [jnp.zeros((start, block_size, block_size), jnp.bfloat16), second_inverse], axis=0
    )
    pivot_inverse = jnp.where(early[:, None, None], pivot_first, pivot_second)
    factor_first = jnp.concatenate(
        [upper_rows, jnp.zeros((start, slot_count, block_size, block_size), jnp.bfloat16)], axis=0
    )
    factor_second = jnp.concatenate(
        [jnp.zeros((start, slot_count, block_size, block_size), jnp.bfloat16), lower_factor], axis=0
    )
    factor_blocks = jnp.where(early[:, None, None, None], factor_first, factor_second)
    return (pivot_inverse, factor_blocks)


def solution(mesh):
    in_specs = (
        P(("row", "col"), None, None),
        P(("row", "col"), None, None, None),
        P(("row", "col"), None),
        P(("row", "col")),
    )
    out_specs = (P(("row", "col"), None, None), P(("row", "col"), None, None, None))
    return jax.shard_map(shards, mesh=mesh, in_specs=in_specs, out_specs=out_specs, check_vma=False)
```

profile of v0, /device:TPU:409, one launch (start us, length us, event | category | flops | bytes accessed | tf_op | source)
XLA Modules:
  0.0 158.0 jit_solution(4676488715472981966)
XLA Ops:
  1.4 1.1 fusion.7
  2.7 1.6 %fusion.17 = f32[6,128,128]{2,1,0:T(8,128)S(1)} fusion(f32[6]{0:T(128)S(1)} %mul.44, bf16[8,128,128]{2,1,0:T(8,128)(2,1)} %param.4), kind=kOutput, calls=%fused_computation.47 | convolution fusion | flops 151191552 | bytes 786456 | tf_op jit(solution)/shard_map/nij,njk->nik/dot_general | solution.py:31
  8.2 1.2 fusion.41
  10.3 2.6 %collective-permute-start = (bf16[1,1,6,7,128,128]{4,5,2,3,1,0:T(8,128)(2,1)S(1)}, bf16[1,1,6,7,128,128]{4,5,2,3,1,0:T(8,128)(2,1)S(1)}, u32[]{:S(2)}, u32[]{:S(2)}) collective-permute-start(bf16[1,1,6,7,128,128]{4,5,2,3,1,0:T(8,128)(2,1)S(1)} %maximum_bitcast_fusion), channel_id=1, source_target_pairs={{16,0},{32,16},{48,32},{64,48},{80,64},{96,80},{112,96},{128,112},... | collective-permute-start | bytes 4128776 | tf_op jit(solution)/shard_map/ppermute | solution.py:20
  12.9 5.1 %collective-permute-start.1 = (bf16[1,1,6,7,128,128]{4,5,2,3,1,0:T(8,128)(2,1)S(1)}, bf16[1,1,6,7,128,128]{4,5,2,3,1,0:T(8,128)(2,1)S(1)}, u32[]{:S(2)}, u32[]{:S(2)}) collective-permute-start(bf16[1,1,6,7,128,128]{4,5,2,3,1,0:T(8,128)(2,1)S(1)} %maximum_bitcast_fusion), channel_id=1, source_target_pairs={{0,16},{16,32},{32,48},{48,64},{64,80},{80,96},{96,112},{112,128},... | collective-permute-start | bytes 4128776 | tf_op jit(solution)/shard_map/ppermute | solution.py:19
  18.0 14.1 %collective-permute-done = bf16[1,1,6,7,128,128]{4,5,2,3,1,0:T(8,128)(2,1)S(1)} collective-permute-done((bf16[1,1,6,7,128,128]{4,5,2,3,1,0:T(8,128)(2,1)S(1)}, bf16[1,1,6,7,128,128]{4,5,2,3,1,0:T(8,128)(2,1)S(1)}, u32[]{:S(2)}, u32[]{:S(2)}) %collective-permute-start) | collective-permute-done | bytes 1376288 | tf_op jit(solution)/shard_map/ppermute | solution.py:20
  32.0 1.2 collective-permute-done.1
  33.2 2.2 %pad_maximum_fusion = bf16[3,1,6,7,128,128]{4,5,2,3,1,0:T(8,128)(2,1)} fusion(bf16[1,1,6,7,128,128]{4,5,2,3,1,0:T(8,128)(2,1)S(1)} %collective-permute-done, bf16[1,1,6,7,128,128]{4,5,2,3,1,0:T(8,128)(2,1)S(1)} %maximum_bitcast_fusion, bf16[1,1,6,7,128,128]{4,5,2,3,1,0:T(8,128)(2,1)S(1)} %collective-permute-done.1), kind=kLoop, calls=%fused_computation.1 | loop fusion | flops 4128768 | bytes 8257536 | tf_op jit(solution)/shard_map/concatenate | solution.py:21
  35.4 3.8 %collective-permute-start.2 = (bf16[3,1,6,7,128,128]{4,5,2,3,1,0:T(8,128)(2,1)}, bf16[3,1,6,7,128,128]{4,5,2,3,1,0:T(8,128)(2,1)}, u32[]{:S(2)}, u32[]{:S(2)}) collective-permute-start(bf16[3,1,6,7,128,128]{4,5,2,3,1,0:T(8,128)(2,1)} %pad_maximum_fusion), channel_id=1, source_target_pairs={{1,0},{2,1},{3,2},{4,3},{5,4},{6,5},{7,6},{8,7},{9,8},{10,9},{11,1... | collective-permute-start | bytes 12386312 | tf_op jit(solution)/shard_map/ppermute | solution.py:20
  39.2 2.1 %collective-permute-start.3 = (bf16[3,1,6,7,128,128]{4,5,2,3,1,0:T(8,128)(2,1)}, bf16[3,1,6,7,128,128]{4,5,2,3,1,0:T(8,128)(2,1)}, u32[]{:S(2)}, u32[]{:S(2)}) collective-permute-start(bf16[3,1,6,7,128,128]{4,5,2,3,1,0:T(8,128)(2,1)} %pad_maximum_fusion), channel_id=1, source_target_pairs={{0,1},{1,2},{2,3},{3,4},{4,5},{5,6},{6,7},{7,8},{8,9},{9,10},{10,1... | collective-permute-start | bytes 12386312 | tf_op jit(solution)/shard_map/ppermute | solution.py:19
  41.5 1.1 fusion.45
  43.4 0.8 fusion.14
  44.2 84.6 %collective-permute-done.2 = bf16[3,1,6,7,128,128]{4,5,2,3,1,0:T(8,128)(2,1)} collective-permute-done((bf16[3,1,6,7,128,128]{4,5,2,3,1,0:T(8,128)(2,1)}, bf16[3,1,6,7,128,128]{4,5,2,3,1,0:T(8,128)(2,1)}, u32[]{:S(2)}, u32[]{:S(2)}) %collective-permute-start.2) | collective-permute-done | bytes 4128800 | tf_op jit(solution)/shard_map/ppermute | solution.py:20
  128.7 1.4 slice_bitcast_fusion.1
  130.2 3.4 %collective-permute-done.3 = bf16[3,1,6,7,128,128]{4,5,2,3,1,0:T(8,128)(2,1)} collective-permute-done((bf16[3,1,6,7,128,128]{4,5,2,3,1,0:T(8,128)(2,1)}, bf16[3,1,6,7,128,128]{4,5,2,3,1,0:T(8,128)(2,1)}, u32[]{:S(2)}, u32[]{:S(2)}) %collective-permute-start.3) | collective-permute-done | bytes 4128800 | tf_op jit(solution)/shard_map/ppermute | solution.py:19
  133.6 1.4 slice_bitcast_fusion
  135.1 0.8 fusion.15
  136.7 0.8 fusion.10
  138.2 4.3 %gather_fusion = bf16[36,2,128,128]{2,3,1,0:T(8,128)(2,1)} fusion(bf16[6,6,2,128,128]{3,4,1,2,0:T(8,128)(2,1)} %fusion.12, s32[36]{0:T(128)S(1)} %reshape.21), kind=kCustom, calls=%fused_computation | custom fusion | bytes 4718880 | tf_op jit(solution)/shard_map/gather | solution.py:65
  142.5 2.0 %abs_reduce_fusion = (f32[6,128]{1,0:T(8,128)S(1)}, f32[6,128]{1,0:T(8,128)S(1)}, f32[6,128,128]{2,1,0:T(8,128)S(1)}) fusion(bf16[6,6,128,128]{3,2,1,0:T(8,128)(2,1)S(1)} %copy-done.4, bf16[6,6,2,128,128]{3,4,2,1,0:T(8,128)(2,1)} %bitcast.93, bf16[8,128,128]{2,1,0:T(8,128)(2,1)S(1)} %copy-done.2), kind=kOutput, calls=%fused_computation.45 | convolution fusion | flops 151484928 | bytes 2955264 | tf_op jit(solution)/shard_map/qkij,qkjl->qil/dot_general | solution.py:72
  144.6 2.0 %convolution_convert_fusion = bf16[6,6,128,128]{2,3,0,1:T(8,128)(2,1)} fusion(bf16[6,6,128,128]{3,2,1,0:T(8,128)(2,1)S(1)} %copy-done.4, bf16[6,6,2,128,128]{3,4,2,1,0:T(8,128)(2,1)S(1)} %bitcast.94), kind=kOutput, calls=%fused_computation.4 | convolution fusion | flops 151584768 | bytes 3538944 | tf_op jit(solution)/shard_map/qkij,qkjl->qkil/dot_general | solution.py:69
  146.8 1.0 fusion.18
  147.8 0.9 convolution_subtract_fusion.3
  148.7 0.9 fusion.48
  149.6 0.8 convolution_subtract_fusion.2
  150.4 0.9 fusion.49
  151.4 0.8 convolution_subtract_fusion.1
  152.2 0.9 fusion.50
  153.1 0.8 fusion.6
  154.1 0.9 copy.55
  154.9 1.5 pad_select_fusion
  156.4 1.6 copy.56
  (43 shorter events, 8.6 us)
Async XLA Ops:
  0.6 3.7 %copy-start.2 = (bf16[8,128,128]{2,1,0:T(8,128)(2,1)S(1)}, bf16[8,128,128]{2,1,0:T(8,128)(2,1)}, u32[]{:S(2)}) copy-start(bf16[8,128,128]{2,1,0:T(8,128)(2,1)} %param.4) | copy-start | bytes 786436
  6.5 1.7 %copy-start = (bf16[8,6,128,128]{3,2,1,0:T(8,128)(2,1)S(1)}, bf16[8,6,128,128]{3,2,1,0:T(8,128)(2,1)}, u32[]{:S(2)}) copy-start(bf16[8,6,128,128]{3,2,1,0:T(8,128)(2,1)} %param.5) | copy-start | bytes 4718596
  10.3 31.1 %copy-start.5 = (s32[8,6]{1,0:T(8,128)S(1)}, s32[8,6]{1,0:T(8,128)}, u32[]{:S(2)}) copy-start(s32[8,6]{1,0:T(8,128)} %param.6) | copy-start | bytes 580
  10.3 31.2 %copy-start.6 = (s32[8]{0:T(128)S(1)}, s32[8]{0:T(128)}, u32[]{:S(2)}) copy-start(s32[8]{0:T(128)} %param.7) | copy-start | bytes 100
  10.3 21.7 %collective-permute-start = (bf16[1,1,6,7,128,128]{4,5,2,3,1,0:T(8,128)(2,1)S(1)}, bf16[1,1,6,7,128,128]{4,5,2,3,1,0:T(8,128)(2,1)S(1)}, u32[]{:S(2)}, u32[]{:S(2)}) collective-permute-start(bf16[1,1,6,7,128,128]{4,5,2,3,1,0:T(8,128)(2,1)S(1)} %maximum_bitcast_fusion), channel_id=1, source_target_pairs={{16,0},{32,16},{48,32},{64,48},{80,64},{96,80},{112,96},{128,112},... | collective-permute-start | bytes 4128776 | tf_op jit(solution)/shard_map/ppermute | solution.py:20
  12.9 20.3 %collective-permute-start.1 = (bf16[1,1,6,7,128,128]{4,5,2,3,1,0:T(8,128)(2,1)S(1)}, bf16[1,1,6,7,128,128]{4,5,2,3,1,0:T(8,128)(2,1)S(1)}, u32[]{:S(2)}, u32[]{:S(2)}) collective-permute-start(bf16[1,1,6,7,128,128]{4,5,2,3,1,0:T(8,128)(2,1)S(1)} %maximum_bitcast_fusion), channel_id=1, source_target_pairs={{0,16},{16,32},{32,48},{48,64},{64,80},{80,96},{96,112},{112,128},... | collective-permute-start | bytes 4128776 | tf_op jit(solution)/shard_map/ppermute | solution.py:19
  32.0 3.3 %copy-start.3 = (bf16[1,1,6,7,128,128]{4,5,2,3,1,0:T(8,128)(2,1)}, bf16[1,1,6,7,128,128]{4,5,2,3,1,0:T(8,128)(2,1)S(1)}, u32[]{:S(2)}) copy-start(bf16[1,1,6,7,128,128]{4,5,2,3,1,0:T(8,128)(2,1)S(1)} %collective-permute-done) | copy-start | bytes 4128772
  35.4 93.3 %collective-permute-start.2 = (bf16[3,1,6,7,128,128]{4,5,2,3,1,0:T(8,128)(2,1)}, bf16[3,1,6,7,128,128]{4,5,2,3,1,0:T(8,128)(2,1)}, u32[]{:S(2)}, u32[]{:S(2)}) collective-permute-start(bf16[3,1,6,7,128,128]{4,5,2,3,1,0:T(8,128)(2,1)} %pad_maximum_fusion), channel_id=1, source_target_pairs={{1,0},{2,1},{3,2},{4,3},{5,4},{6,5},{7,6},{8,7},{9,8},{10,9},{11,1... | collective-permute-start | bytes 12386312 | tf_op jit(solution)/shard_map/ppermute | solution.py:20
  39.2 94.4 %collective-permute-start.3 = (bf16[3,1,6,7,128,128]{4,5,2,3,1,0:T(8,128)(2,1)}, bf16[3,1,6,7,128,128]{4,5,2,3,1,0:T(8,128)(2,1)}, u32[]{:S(2)}, u32[]{:S(2)}) collective-permute-start(bf16[3,1,6,7,128,128]{4,5,2,3,1,0:T(8,128)(2,1)} %pad_maximum_fusion), channel_id=1, source_target_pairs={{0,1},{1,2},{2,3},{3,4},{4,5},{5,6},{6,7},{7,8},{8,9},{9,10},{10,1... | collective-permute-start | bytes 12386312 | tf_op jit(solution)/shard_map/ppermute | solution.py:19
  138.2 4.3 %copy-start.4 = (bf16[6,6,128,128]{3,2,1,0:T(8,128)(2,1)S(1)}, bf16[6,6,128,128]{3,2,1,0:T(8,128)(2,1)}, u32[]{:S(2)}) copy-start(bf16[6,6,128,128]{3,2,1,0:T(8,128)(2,1)} %get-tuple-element.13) | copy-start | bytes 3538948
  142.5 2.0 %copy-start.1 = (bf16[36,2,128,128]{2,3,1,0:T(8,128)(2,1)S(1)}, bf16[36,2,128,128]{2,3,1,0:T(8,128)(2,1)}, u32[]{:S(2)}) copy-start(bf16[36,2,128,128]{2,3,1,0:T(8,128)(2,1)} %gather_fusion) | copy-start | bytes 7077892
where the time goes:
time: 158 us
  waiting for transfers between devices  103 us (65%)
  matrix products  17.1 us (11%)
  starting transfers between devices  13.6 us (9%)
  other arithmetic  12.1 us (8%)
  local copies, waits for them, and re-layouts  11 us (7%)
    ppermute x2, waiting for transfers between devices, padded(): after = lax.ppermute(initial, axis, down)  98.6 us
    ppermute x2, starting transfers between devices, padded(): before = lax.ppermute(last, axis, up)  7.19 us
    dot_general x8, matrix products, approx_inverse(): jnp.einsum('nij,njk->nik', matrix, iterate, precision=lax.Precision.HIGHEST)  7.06 us
    ppermute x2, starting transfers between devices, padded(): after = lax.ppermute(initial, axis, down)  6.42 us
    dot_general x8, matrix products, approx_inverse(): jnp.einsum('nij,njk->nik', iterate, product, precision=lax.Precision.HIGH...  5.47 us
    ppermute x2, waiting for transfers between devices, padded(): before = lax.ppermute(last, axis, up)  4.61 us
    gather x1, local copies, waits for them, and re-layouts, shards(): picked = table[jnp.arange(slot_count)[None, :], local_rows]  4.3 us
    unnamed x5, other arithmetic  3.96 us
  transfers between devices with their start and end apart: 4, of which 4 were waited for; matrix products, arithmetic and copies ran while one was open for 3% of the time, Pallas kernels for 0%

commit v1 on v0

v1 whole, which is shorter than its diff:
```python
import jax
import jax.numpy as jnp
from jax import lax
from jax.experimental import pallas as pl
from jax.experimental.pallas import tpu as pltpu
from jax.sharding import PartitionSpec as P

NS_STEPS = 4
MIRROR = (1, 0, 3, 2, 5, 4)
MOVES = ((1, 0), (-1, 0), (0, 1), (0, -1))
REMOTE = len(MOVES)
MESH = pl.DeviceIdType.MESH
VMEM_LIMIT = 48 * 1024 * 1024


def dot32(left, right):
    return jnp.dot(left, right, preferred_element_type=jnp.float32)


def split(value):
    high = value.astype(jnp.bfloat16)
    return high, (value - high.astype(jnp.float32)).astype(jnp.bfloat16)


def inverses(matrices, exact):
    size = matrices[0].shape[0]
    row_id = lax.broadcasted_iota(jnp.int32, (size, size), 0)
    col_id = lax.broadcasted_iota(jnp.int32, (size, size), 1)
    identity = (row_id == col_id).astype(jnp.float32)
    lefts, iterates = [], []
    for matrix in matrices:
        magnitude = jnp.abs(matrix)
        column_norm = jnp.max(jnp.sum(magnitude, axis=0, keepdims=True), axis=1, keepdims=True)
        row_norm = jnp.max(jnp.sum(magnitude, axis=1, keepdims=True), axis=0, keepdims=True)
        iterates.append(matrix.T * (1.0 / (column_norm * row_norm)))
        high, low = split(matrix)
        lefts.append(jnp.concatenate([high, high] if exact else [high, high, low], axis=1))
    for _ in range(NS_STEPS):
        halves = [split(iterate) for iterate in iterates]
        rests = [
            identity - dot32(left, jnp.concatenate([high, low] if exact else [high, low, high], axis=0))
            for left, (high, low) in zip(lefts, halves)
        ]
        rests = [rest.astype(jnp.bfloat16) for rest in rests]
        iterates = [
            iterate + dot32(jnp.concatenate([high, low], axis=1), jnp.concatenate([rest, rest], axis=0))
            for iterate, (high, low), rest in zip(iterates, halves, rests)
        ]
    return [iterate.astype(jnp.bfloat16) for iterate in iterates]


def exchange(sizes, capacity, diag_ref, off_ref, inv_ref, got_off, got_inv, send_sem, recv_sem):
    here = (lax.axis_index("row"), lax.axis_index("col"))
    there, exists = [], []
    for move in MOVES:
        target = tuple(here[axis] + move[axis] for axis in range(2))
        axis = 0 if move[0] != 0 else 1
        there.append(target)
        exists.append((target[axis] < sizes[axis]) if move[axis] > 0 else (target[axis] >= 0))

    barrier = pltpu.get_barrier_semaphore()
    for side in range(REMOTE):
        @pl.when(exists[side])
        def _():
            pl.semaphore_signal(barrier, inc=1, device_id=there[side], device_id_type=MESH)
    pl.semaphore_wait(barrier, sum(flag.astype(jnp.int32) for flag in exists))

    def outgoing(kind, side):
        source, landing = ((off_ref.at[pl.ds(0, capacity), side], got_off), (inv_ref, got_inv))[kind]
        return pltpu.make_async_remote_copy(
            src_ref=source,
            dst_ref=landing.at[MIRROR[side]],
            send_sem=send_sem.at[kind, side],
            recv_sem=recv_sem.at[kind, MIRROR[side]],
            device_id=there[side],
            device_id_type=MESH,
        )

    def incoming(kind, side):
        landing = (got_off, got_inv)[kind]
        return pltpu.make_async_remote_copy(
            src_ref=landing.at[side],
            dst_ref=landing.at[side],
            send_sem=send_sem.at[kind, side],
            recv_sem=recv_sem.at[kind, side],
            device_id=there[side],
            device_id_type=MESH,
        )

    for side in (2, 3, 0, 1):
        @pl.when(exists[side])
        def _():
            outgoing(0, side).start()

    found = inverses([diag_ref[i].astype(jnp.float32) for i in range(capacity)], True)
    for i in range(capacity):
        inv_ref[i] = found[i]
    for side in (2, 3, 0, 1):
        @pl.when(exists[side])
        def _():
            outgoing(1, side).start()
    for side in range(REMOTE):
        @pl.when(exists[side])
        def _():
            for kind in range(2):
                outgoing(kind, side).wait_send()
                incoming(kind, side).wait_recv()


def finish(capacity, named_ref, level_ref, diag_ref, off_ref, inv_ref, got_off, got_inv, pivot_ref, factor_ref):
    rows, slots, size, _ = off_ref.shape
    start = rows - capacity
    zero = jnp.zeros((size, size), jnp.bfloat16)

    def scaled(i):
        wide = dot32(inv_ref[i], jnp.concatenate([off_ref[i, k] for k in range(slots)], axis=1))
        wide = wide.astype(jnp.bfloat16)
        return [
            jnp.where(named_ref[i, k] >= 0, wide[:, k * size : (k + 1) * size], zero)
            for k in range(slots)
        ]

    pivots = []
    for q in range(start, rows):
        lowers, facing = [], []
        for k in range(slots):
            named = named_ref[q, k]
            live = named >= 0
            local = jnp.minimum(lax.rem(jnp.maximum(named, 0), rows), capacity - 1)
            if k < REMOTE:
                across, faced = got_inv[k, local], got_off[k, local]
            else:
                across, faced = inv_ref[local], off_ref[local, MIRROR[k]]
            across = jnp.where(live, across, zero)
            mine = jnp.where(live, off_ref[q, k], zero)
            lowers.append(dot32(mine, across).astype(jnp.bfloat16))
            facing.append(jnp.where(live, faced, zero))
        schur = dot32(jnp.concatenate(lowers, axis=1), jnp.concatenate(facing, axis=0))
        pivots.append(diag_ref[q].astype(jnp.float32) - schur)
        if q < capacity:
            early = level_ref[q] == 0
            uppers = scaled(q)
            for k in range(slots):
                factor_ref[q, k] = jnp.where(early, uppers[k], lowers[k])
        else:
            for k in range(slots):
                factor_ref[q, k] = lowers[k]
    for i in range(start):
        uppers = scaled(i)
        for k in range(slots):
            factor_ref[i, k] = uppers[k]
        pivot_ref[i] = inv_ref[i]
    second = inverses(pivots, False)
    for q in range(start, rows):
        if q < capacity:
            pivot_ref[q] = jnp.where(level_ref[q] == 0, inv_ref[q], second[q - start])
        else:
            pivot_ref[q] = second[q - start]


def solution(mesh):
    sizes = (mesh.shape["row"], mesh.shape["col"])

    def shards(diag_blocks, off_blocks, neighbors, levels):
        rows, slots, size, _ = off_blocks.shape
        capacity = 3 * rows // 4
        dtype = jnp.bfloat16
        anywhere = pl.BlockSpec(memory_space=pl.ANY)
        vmem = pl.BlockSpec(memory_space=pltpu.VMEM)
        smem = pl.BlockSpec(memory_space=pltpu.SMEM)
        got = jax.ShapeDtypeStruct((REMOTE, capacity, size, size), dtype)
        inverse, got_off, got_inv = pl.pallas_call(
            lambda *refs: exchange(sizes, capacity, *refs),
            name="exchange",
            out_shape=(jax.ShapeDtypeStruct((capacity, size, size), dtype), got, got),
            in_specs=[vmem, anywhere],
            out_specs=(vmem, anywhere, anywhere),
            scratch_shapes=[
                pltpu.SemaphoreType.DMA((2, REMOTE)),
                pltpu.SemaphoreType.DMA((2, REMOTE)),
            ],
            compiler_params=pltpu.CompilerParams(
                collective_id=0, has_side_effects=True, vmem_limit_bytes=VMEM_LIMIT
            ),
        )(diag_blocks, off_blocks)
        return pl.pallas_call(
            lambda *refs: finish(capacity, *refs),
            name="finish",
            out_shape=(
                jax.ShapeDtypeStruct((rows, size, size), dtype),
                jax.ShapeDtypeStruct((rows, slots, size, size), dtype),
            ),
            in_specs=[smem, smem] + [vmem] * 5,
            out_specs=(vmem, vmem),
            compiler_params=pltpu.CompilerParams(vmem_limit_bytes=VMEM_LIMIT),
        )(neighbors, levels, diag_blocks, off_blocks, inverse, got_off, got_inv)

    blocks = P(("row", "col"), None, None)
    wide = P(("row", "col"), None, None, None)
    in_specs = (blocks, wide, P(("row", "col"), None), P(("row", "col")))
    return jax.shard_map(shards, mesh=mesh, in_specs=in_specs, out_specs=(blocks, wide), check_vma=False)
```

time: 158 us -> 24.1 us (0.15)
  the two profiles are of different devices: /device:TPU:409 before, /device:TPU:1 now
where the time goes in v1:
time: 24.1 us; the launch traced here: 24 us
  Pallas kernels  20.9 us (87%)
  local copies, waits for them, and re-layouts  2.36 us (10%)
  between operations  0.66 us (3%)
    pallas_call x1, Pallas kernels, shards(): pl.pallas_call(lambda *refs: exchange(sizes, capacity, *refs), name='exch...  16.5 us
    pallas_call x1, Pallas kernels, shards(): pl.pallas_call(lambda *refs: finish(capacity, *refs), name='finish', out_...  4.4 us
    unnamed x8, local copies, waits for them, and re-layouts  2.36 us

profile of v1, /device:TPU:1, one launch (start us, length us, event | category | flops | bytes accessed | tf_op | source)
XLA Modules:
  0.0 24.0 jit_solution(14737436873578614801)
XLA Ops:
  0.6 0.0 copy-start
  0.6 1.4 %copy-done = bf16[8,6,128,128]{3,2,1,0:T(8,128)(2,1)S(1)} copy-done((bf16[8,6,128,128]{3,2,1,0:T(8,128)(2,1)S(1)}, bf16[8,6,128,128]{3,2,1,0:T(8,128)(2,1)}, u32[]{:S(2)}) %copy-start) | copy-done | bytes 1572888
  2.0 0.0 copy-start.1
  2.0 0.9 %copy-done.1 = bf16[8,128,128]{2,1,0:T(8,128)(2,1)S(1)} copy-done((bf16[8,128,128]{2,1,0:T(8,128)(2,1)S(1)}, bf16[8,128,128]{2,1,0:T(8,128)(2,1)}, u32[]{:S(2)}) %copy-start.1) | copy-done | bytes 262168
  3.0 0.0 copy-start.2
  3.0 0.0 copy-start.3
  3.0 16.5 %exchange.1 = (bf16[6,128,128]{2,1,0:T(8,128)(2,1)S(1)}, bf16[4,6,128,128]{3,2,1,0:T(8,128)(2,1)S(1)}, bf16[4,6,128,128]{3,2,1,0:T(8,128)(2,1)S(1)}) custom-call(bf16[8,128,128]{2,1,0:T(8,128)(2,1)S(1)} %copy-done.1, bf16[8,6,128,128]{3,2,1,0:T(8,128)(2,1)S(1)} %copy-done), custom_call_target="tpu_custom_call" | custom-call | tf_op jit(solution)/shard_map/exchange/pallas_call | solution.py:172
  19.5 0.0 copy-done.2
  19.5 0.0 copy-done.3
  19.6 4.4 %finish.1 = (bf16[8,128,128]{2,1,0:T(8,128)(2,1)}, bf16[8,6,128,128]{3,2,1,0:T(8,128)(2,1)}) custom-call(s32[8,6]{1,0:T(8,128)S(1)} %copy-done.2, s32[8]{0:T(128)S(1)} %copy-done.3, bf16[8,128,128]{2,1,0:T(8,128)(2,1)S(1)} %copy-done.1, bf16[8,6,128,128]{3,2,1,0:T(8,128)(2,1)S(1)} %copy-done, bf16[6,128,128]{2,1,0:T(8,128)(2,1)S(1)} %get-tuple-element.5.refs_4_, ...), custom_call_target="tpu_custom_call" | custom-call | tf_op jit(solution)/shard_map/finish/pallas_call | solution.py:186
Async XLA Ops:
  0.6 1.4 %copy-start = (bf16[8,6,128,128]{3,2,1,0:T(8,128)(2,1)S(1)}, bf16[8,6,128,128]{3,2,1,0:T(8,128)(2,1)}, u32[]{:S(2)}) copy-start(bf16[8,6,128,128]{3,2,1,0:T(8,128)(2,1)} %refs_3_.1) | copy-start | bytes 4718596
  2.0 0.9 %copy-start.1 = (bf16[8,128,128]{2,1,0:T(8,128)(2,1)S(1)}, bf16[8,128,128]{2,1,0:T(8,128)(2,1)}, u32[]{:S(2)}) copy-start(bf16[8,128,128]{2,1,0:T(8,128)(2,1)} %refs_2_.1) | copy-start | bytes 786436
  3.0 16.5 %copy-start.2 = (s32[8,6]{1,0:T(8,128)S(1)}, s32[8,6]{1,0:T(8,128)}, u32[]{:S(2)}) copy-start(s32[8,6]{1,0:T(8,128)} %refs_0_.3) | copy-start | bytes 580
  3.0 16.6 %copy-start.3 = (s32[8]{0:T(128)S(1)}, s32[8]{0:T(128)}, u32[]{:S(2)}) copy-start(s32[8]{0:T(128)} %refs_1_.3) | copy-start | bytes 100

commit v2 on v1

v2 whole, which is shorter than its diff:
```python
import jax
import jax.numpy as jnp
from jax import lax
from jax.experimental import pallas as pl
from jax.experimental.pallas import tpu as pltpu
from jax.sharding import PartitionSpec as P

NS_STEPS = 4
MIRROR = (1, 0, 3, 2, 5, 4)
MOVES = ((1, 0), (-1, 0), (0, 1), (0, -1))
REMOTE = len(MOVES)
MESH = pl.DeviceIdType.MESH
VMEM_LIMIT = 40 * 1024 * 1024
SIDEWAYS = (0, 1)
ALONG = (2, 3)
INSIDE = (4, 5)


def dot32(left, right):
    return jnp.dot(left, right, preferred_element_type=jnp.float32)


def split(value):
    high = value.astype(jnp.bfloat16)
    return high, (value - high.astype(jnp.float32)).astype(jnp.bfloat16)


def inverses(matrices, exact):
    size = matrices[0].shape[0]
    row_id = lax.broadcasted_iota(jnp.int32, (size, size), 0)
    col_id = lax.broadcasted_iota(jnp.int32, (size, size), 1)
    identity = (row_id == col_id).astype(jnp.float32)
    lefts, iterates = [], []
    for matrix in matrices:
        magnitude = jnp.abs(matrix)
        column_norm = jnp.max(jnp.sum(magnitude, axis=0, keepdims=True), axis=1, keepdims=True)
        row_norm = jnp.max(jnp.sum(magnitude, axis=1, keepdims=True), axis=0, keepdims=True)
        iterates.append(matrix.T * (1.0 / (column_norm * row_norm)))
        high, low = split(matrix)
        lefts.append(jnp.concatenate([high, high] if exact else [high, high, low], axis=1))
    for _ in range(NS_STEPS):
        halves = [split(iterate) for iterate in iterates]
        rests = [
            identity - dot32(left, jnp.concatenate([high, low] if exact else [high, low, high], axis=0))
            for left, (high, low) in zip(lefts, halves)
        ]
        rests = [rest.astype(jnp.bfloat16) for rest in rests]
        iterates = [
            iterate + dot32(jnp.concatenate([high, low], axis=1), jnp.concatenate([rest, rest], axis=0))
            for iterate, (high, low), rest in zip(iterates, halves, rests)
        ]
    return [iterate.astype(jnp.bfloat16) for iterate in iterates]


def picker(named_ref, rows, capacity):
    def pick(q, k):
        named = named_ref[q, k]
        local = jnp.minimum(lax.rem(jnp.maximum(named, 0), rows), capacity - 1)
        return named >= 0, local

    return pick


def exchange(
    sizes, capacity, diag_hbm, off_hbm, named_hbm, level_hbm,
    inv_ref, part_ref, rest_ref, mine_ref, far_off, far_inv,
    diag_ref, off_ref, named_ref, level_ref, near_off, near_inv, local_sem, send_sem, recv_sem,
):
    rows, slots, size, _ = off_ref.shape
    start = rows - capacity
    zero = jnp.zeros((size, size), jnp.bfloat16)
    here = (lax.axis_index("row"), lax.axis_index("col"))
    there, exists = [], []
    for move in MOVES:
        target = tuple(here[axis] + move[axis] for axis in range(2))
        axis = 0 if move[0] != 0 else 1
        there.append(target)
        exists.append((target[axis] < sizes[axis]) if move[axis] > 0 else (target[axis] >= 0))

    barrier = pltpu.get_barrier_semaphore()
    for side in range(REMOTE):
        @pl.when(exists[side])
        def _():
            pl.semaphore_signal(barrier, inc=1, device_id=there[side], device_id_type=MESH)
    loads = [
        pltpu.make_async_copy(source, target, local_sem.at[i])
        for i, (source, target) in enumerate([
            (diag_hbm, diag_ref),
            (off_hbm, off_ref),
            (named_hbm, named_ref),
            (level_hbm, level_ref),
            (off_hbm.at[pl.ds(start, capacity), pl.ds(ALONG[0], 2)], mine_ref),
        ])
    ]
    for load in loads:
        load.start()
    pl.semaphore_wait(barrier, sum(flag.astype(jnp.int32) for flag in exists))

    def landing(kind, side):
        if side in ALONG:
            return (far_off, far_inv)[kind].at[side - ALONG[0]]
        return (near_off, near_inv)[kind].at[side]

    def transfer(kind, source, side, arrives):
        return pltpu.make_async_remote_copy(
            src_ref=source,
            dst_ref=landing(kind, arrives),
            send_sem=send_sem.at[kind, side],
            recv_sem=recv_sem.at[kind, arrives],
            device_id=there[side],
            device_id_type=MESH,
        )

    def outgoing(kind, side):
        source = inv_ref if kind else off_hbm.at[pl.ds(0, capacity), side]
        return transfer(kind, source, side, MIRROR[side])

    def incoming(kind, side):
        return transfer(kind, landing(kind, side), side, side)

    for side in ALONG + SIDEWAYS:
        @pl.when(exists[side])
        def _():
            outgoing(0, side).start()

    loads[0].wait()
    found = inverses([diag_ref[i].astype(jnp.float32) for i in range(capacity)], True)
    for i in range(capacity):
        inv_ref[i] = found[i]
    for side in ALONG + SIDEWAYS:
        @pl.when(exists[side])
        def _():
            outgoing(1, side).start()

    for load in loads[1:]:
        load.wait()
    pick = picker(named_ref, rows, capacity)
    for i in range(capacity):
        upper = dot32(inv_ref[i], jnp.concatenate([off_ref[i, k] for k in range(slots)], axis=1))
        upper = upper.astype(jnp.bfloat16)
        for k in range(slots):
            part_ref[i, k] = jnp.where(
                named_ref[i, k] >= 0, upper[:, k * size : (k + 1) * size], zero
            )

    def absorb(group, before):
        for q in range(start, rows):
            lowers, facing = [], []
            for k in group:
                live, local = pick(q, k)
                if k in INSIDE:
                    across, faced = inv_ref[local], off_ref[local, MIRROR[k]]
                else:
                    across, faced = near_inv[k, local], near_off[k, local]
                lower = dot32(
                    jnp.where(live, off_ref[q, k], zero), jnp.where(live, across, zero)
                ).astype(jnp.bfloat16)
                lowers.append(lower)
                facing.append(jnp.where(live, faced, zero))
                if q < capacity:
                    part_ref[q, k] = jnp.where(level_ref[q] == 0, part_ref[q, k], lower)
                else:
                    part_ref[q, k] = lower
            schur = dot32(jnp.concatenate(lowers, axis=1), jnp.concatenate(facing, axis=0))
            rest_ref[q - start] = before(q) - schur

    absorb(INSIDE, lambda q: diag_ref[q].astype(jnp.float32))
    for side in SIDEWAYS:
        @pl.when(exists[side])
        def _():
            for kind in range(2):
                incoming(kind, side).wait_recv()
    absorb(SIDEWAYS, lambda q: rest_ref[q - start])
    for side in ALONG:
        @pl.when(exists[side])
        def _():
            for kind in range(2):
                incoming(kind, side).wait_recv()
    for side in range(REMOTE):
        @pl.when(exists[side])
        def _():
            for kind in range(2):
                outgoing(kind, side).wait_send()


def finish(
    capacity, named_ref, level_ref, inv_ref, part_ref, rest_ref, mine_ref, far_off, far_inv,
    pivot_hbm, factor_hbm, pivot_ref, lower_ref, sems,
):
    rows, slots, size, _ = part_ref.shape
    start = rows - capacity
    zero = jnp.zeros((size, size), jnp.bfloat16)
    late = pl.ds(start, capacity)
    soon = pl.ds(0, start)
    stores = [
        pltpu.make_async_copy(source, target, sems.at[i])
        for i, (source, target) in enumerate([
            (part_ref.at[soon], factor_hbm.at[soon]),
            (part_ref.at[late, pl.ds(SIDEWAYS[0], 2)], factor_hbm.at[late, pl.ds(SIDEWAYS[0], 2)]),
            (part_ref.at[late, pl.ds(INSIDE[0], 2)], factor_hbm.at[late, pl.ds(INSIDE[0], 2)]),
            (inv_ref.at[soon], pivot_hbm.at[soon]),
            (lower_ref, factor_hbm.at[late, pl.ds(ALONG[0], 2)]),
            (pivot_ref, pivot_hbm.at[late]),
        ])
    ]
    for store in stores[:4]:
        store.start()
    pick = picker(named_ref, rows, capacity)
    pivots = []
    for q in range(start, rows):
        lowers, facing = [], []
        for j, k in enumerate(ALONG):
            live, local = pick(q, k)
            lower = dot32(
                jnp.where(live, mine_ref[q - start, j], zero), jnp.where(live, far_inv[j, local], zero)
            ).astype(jnp.bfloat16)
            lowers.append(lower)
            facing.append(jnp.where(live, far_off[j, local], zero))
            if q < capacity:
                lower = jnp.where(level_ref[q] == 0, part_ref[q, k], lower)
            lower_ref[q - start, j] = lower
        schur = dot32(jnp.concatenate(lowers, axis=1), jnp.concatenate(facing, axis=0))
        pivots.append(rest_ref[q - start] - schur)
    stores[4].start()
    second = inverses(pivots, False)
    for q in range(start, rows):
        value = second[q - start]
        if q < capacity:
            value = jnp.where(level_ref[q] == 0, inv_ref[q], value)
        pivot_ref[q - start] = value
    stores[5].start()
    for store in stores:
        store.wait()


def solution(mesh):
    sizes = (mesh.shape["row"], mesh.shape["col"])

    def shards(diag_blocks, off_blocks, neighbors, levels):
        rows, slots, size, _ = off_blocks.shape
        capacity = 3 * rows // 4
        block = (size, size)
        hbm = pl.BlockSpec(memory_space=pltpu.HBM)
        vmem = pl.BlockSpec(memory_space=pltpu.VMEM)
        smem = pl.BlockSpec(memory_space=pltpu.SMEM)

        def shape(*lead, dtype=jnp.bfloat16):
            return jax.ShapeDtypeStruct(lead + block, dtype)

        def room(*lead):
            return pltpu.VMEM(lead + block, jnp.bfloat16)

        carried = pl.pallas_call(
            lambda *refs: exchange(sizes, capacity, *refs),
            name="exchange",
            out_shape=(
                shape(capacity),
                shape(rows, slots),
                shape(capacity, dtype=jnp.float32),
                shape(capacity, 2),
                shape(2, capacity),
                shape(2, capacity),
            ),
            in_specs=[hbm] * 4,
            out_specs=(vmem,) * 6,
            scratch_shapes=[
                room(rows),
                room(rows, slots),
                pltpu.SMEM(neighbors.shape, jnp.int32),
                pltpu.SMEM(levels.shape, jnp.int32),
                room(2, capacity),
                room(2, capacity),
                pltpu.SemaphoreType.DMA((5,)),
                pltpu.SemaphoreType.DMA((2, REMOTE)),
                pltpu.SemaphoreType.DMA((2, REMOTE)),
            ],
            compiler_params=pltpu.CompilerParams(
                collective_id=0, has_side_effects=True, vmem_limit_bytes=VMEM_LIMIT
            ),
        )(*[pltpu.with_memory_space_constraint(x, pltpu.HBM) for x in (diag_blocks, off_blocks, neighbors, levels)])
        return pl.pallas_call(
            lambda *refs: finish(capacity, *refs),
            name="finish",
            out_shape=(shape(rows), shape(rows, slots)),
            in_specs=[smem] * 2 + [vmem] * 6,
            out_specs=(hbm, hbm),
            scratch_shapes=[room(capacity), room(capacity, 2), pltpu.SemaphoreType.DMA((6,))],
            compiler_params=pltpu.CompilerParams(vmem_limit_bytes=VMEM_LIMIT),
        )(neighbors, levels, *carried)

    blocks = P(("row", "col"), None, None)
    wide = P(("row", "col"), None, None, None)
    in_specs = (blocks, wide, P(("row", "col"), None), P(("row", "col")))
    return jax.shard_map(shards, mesh=mesh, in_specs=in_specs, out_specs=(blocks, wide), check_vma=False)
```

time: 24.1 us -> 21.2 us (0.88)
  local copies, waits for them, and re-layouts: 2.36 us -> 0.01 us
  Pallas kernels: 20.9 us -> 20.3 us
    unnamed x8 -> x4, local copies, waits for them, and re-layouts: 2.36 us -> 0.01 us
    pallas_call x1, Pallas kernels: 4.4 us -> 3.64 us  [shards(): pl.pallas_call(lambda *refs: finish(capacity, *refs), name='finish', out_...]
where the time goes in v2:
time: 21.2 us; the launch traced here: 21 us
  Pallas kernels  20.3 us (96%)
  between operations  0.67 us (3%)
    pallas_call x1, Pallas kernels, shards(): pl.pallas_call(lambda *refs: exchange(sizes, capacity, *refs), name='exch...  16.7 us
    pallas_call x1, Pallas kernels, shards(): pl.pallas_call(lambda *refs: finish(capacity, *refs), name='finish', out_...  3.64 us

profile of v2, /device:TPU:1, one launch (start us, length us, event | category | flops | bytes accessed | tf_op | source)
XLA Modules:
  0.0 21.0 jit_solution(2277495705767490544)
XLA Ops:
  0.6 0.0 copy-start.1
  0.6 0.0 copy-start
  0.7 16.7 %exchange.1 = (bf16[6,128,128]{2,1,0:T(8,128)(2,1)S(1)}, bf16[8,6,128,128]{3,2,1,0:T(8,128)(2,1)S(1)}, f32[6,128,128]{2,1,0:T(8,128)S(1)}, bf16[6,2,128,128]{3,2...) custom-call(bf16[8,128,128]{2,1,0:T(8,128)(2,1)} %refs_0_.2, ...), custom_call_target="tpu_custom_call" | custom-call | tf_op jit(solution)/shard_map/exchange/pallas_call | solution.py:253
  17.4 0.0 copy-done.1
  17.4 0.0 copy-done
  17.4 3.6 %finish.1 = (bf16[8,128,128]{2,1,0:T(8,128)(2,1)}, bf16[8,6,128,128]{3,2,1,0:T(8,128)(2,1)}) custom-call(s32[8,6]{1,0:T(8,128)S(1)} %copy-done, s32[8]{0:T(128)S(1)} %copy-done.1, bf16[6,128,128]{2,1,0:T(8,128)(2,1)S(1)} %get-tuple-element.8.refs_2_, bf16[8,6,128,128]{3,2,1,0:T(8,128)(2,1)S(1)} %get-tuple-element.9.refs_3_, ...), custom_call_target="tpu_custom_call" | custom-call | tf_op jit(solution)/shard_map/finish/pallas_call | solution.py:281
Async XLA Ops:
  0.6 16.7 %copy-start.1 = (s32[8]{0:T(128)S(1)}, s32[8]{0:T(128)}, u32[]{:S(2)}) copy-start(s32[8]{0:T(128)} %refs_1_.3) | copy-start | bytes 100
  0.6 16.7 %copy-start = (s32[8,6]{1,0:T(8,128)S(1)}, s32[8,6]{1,0:T(8,128)}, u32[]{:S(2)}) copy-start(s32[8,6]{1,0:T(8,128)} %refs_0_.3) | copy-start | bytes 580

commit v3 on v2

--- a/solution.py
+++ b/solution.py
@@ -25,29 +25,29 @@
     return high, (value - high.astype(jnp.float32)).astype(jnp.bfloat16)
 
 
-def inverses(matrices, exact):
+def inverses(matrices, paired):
     size = matrices[0].shape[0]
     row_id = lax.broadcasted_iota(jnp.int32, (size, size), 0)
     col_id = lax.broadcasted_iota(jnp.int32, (size, size), 1)
     identity = (row_id == col_id).astype(jnp.float32)
-    lefts, iterates = [], []
+    iterates = []
     for matrix in matrices:
         magnitude = jnp.abs(matrix)
         column_norm = jnp.max(jnp.sum(magnitude, axis=0, keepdims=True), axis=1, keepdims=True)
         row_norm = jnp.max(jnp.sum(magnitude, axis=1, keepdims=True), axis=0, keepdims=True)
         iterates.append(matrix.T * (1.0 / (column_norm * row_norm)))
-        high, low = split(matrix)
-        lefts.append(jnp.concatenate([high, high] if exact else [high, high, low], axis=1))
+    lefts = [matrix.astype(jnp.bfloat16) for matrix in matrices]
+    if paired:
+        lefts = [jnp.concatenate([left, left], axis=1) for left in lefts]
     for _ in range(NS_STEPS):
-        halves = [split(iterate) for iterate in iterates]
+        halves = [split(iterate) if paired else (iterate.astype(jnp.bfloat16),) for iterate in iterates]
         rests = [
-            identity - dot32(left, jnp.concatenate([high, low] if exact else [high, low, high], axis=0))
-            for left, (high, low) in zip(lefts, halves)
+            (identity - dot32(left, jnp.concatenate(half, axis=0))).astype(jnp.bfloat16)
+            for left, half in zip(lefts, halves)
         ]
-        rests = [rest.astype(jnp.bfloat16) for rest in rests]
         iterates = [
-            iterate + dot32(jnp.concatenate([high, low], axis=1), jnp.concatenate([rest, rest], axis=0))
-            for iterate, (high, low), rest in zip(iterates, halves, rests)
+            iterate + dot32(jnp.concatenate(half, axis=1), jnp.concatenate([rest] * len(half), axis=0))
+            for iterate, half, rest in zip(iterates, halves, rests)
         ]
     return [iterate.astype(jnp.bfloat16) for iterate in iterates]
 
@@ -63,8 +63,8 @@
 
 def exchange(
     sizes, capacity, diag_hbm, off_hbm, named_hbm, level_hbm,
-    inv_ref, part_ref, rest_ref, mine_ref, far_off, far_inv,
-    diag_ref, off_ref, named_ref, level_ref, near_off, near_inv, local_sem, send_sem, recv_sem,
+    inv_ref, part_ref, rest_ref, lower_ref, far_off,
+    far_inv, diag_ref, off_ref, named_ref, level_ref, near_off, near_inv, local_sem, send_sem, recv_sem,
 ):
     rows, slots, size, _ = off_ref.shape
     start = rows - capacity
@@ -89,17 +89,23 @@
             (off_hbm, off_ref),
             (named_hbm, named_ref),
             (level_hbm, level_ref),
-            (off_hbm.at[pl.ds(start, capacity), pl.ds(ALONG[0], 2)], mine_ref),
         ])
     ]
     for load in loads:
         load.start()
     pl.semaphore_wait(barrier, sum(flag.astype(jnp.int32) for flag in exists))
 
+    pieces = (pl.ds(0, capacity - 1), pl.ds(0, capacity), pl.ds(capacity - 1, 1))
+
+    def piece(kind, side):
+        return pieces[1] if side in SIDEWAYS else pieces[kind]
+
     def landing(kind, side):
         if side in ALONG:
-            return (far_off, far_inv)[kind].at[side - ALONG[0]]
-        return (near_off, near_inv)[kind].at[side]
+            target = (far_off, far_inv, far_off)[kind].at[side - ALONG[0]]
+        else:
+            target = (near_off, near_inv)[kind].at[side]
+        return target.at[piece(kind, side)]
 
     def transfer(kind, source, side, arrives):
         return pltpu.make_async_remote_copy(
@@ -112,7 +118,7 @@
         )
 
     def outgoing(kind, side):
-        source = inv_ref if kind else off_hbm.at[pl.ds(0, capacity), side]
+        source = inv_ref if kind == 1 else off_hbm.at[piece(kind, side), side]
         return transfer(kind, source, side, MIRROR[side])
 
     def incoming(kind, side):
@@ -131,6 +137,8 @@
         @pl.when(exists[side])
         def _():
             outgoing(1, side).start()
+            if side in ALONG:
+                outgoing(2, side).start()
 
     for load in loads[1:]:
         load.wait()
@@ -143,24 +151,31 @@
                 named_ref[i, k] >= 0, upper[:, k * size : (k + 1) * size], zero
             )
 
+    def lower_blocks(q, group):
+        lowers = []
+        for k in group:
+            live, local = pick(q, k)
+            if k in INSIDE:
+                across = inv_ref[local]
+            elif k in SIDEWAYS:
+                across = near_inv[k, local]
+            else:
+                across = far_inv[k - ALONG[0], local]
+            lower = dot32(off_ref[q, k], jnp.where(live, across, zero)).astype(jnp.bfloat16)
+            lowers.append(lower)
+            if q < capacity:
+                lower = jnp.where(level_ref[q] == 0, part_ref[q, k], lower)
+            part_ref[q, k] = lower
+        return lowers
+
     def absorb(group, before):
         for q in range(start, rows):
-            lowers, facing = [], []
+            facing = []
             for k in group:
                 live, local = pick(q, k)
-                if k in INSIDE:
-                    across, faced = inv_ref[local], off_ref[local, MIRROR[k]]
-                else:
-                    across, faced = near_inv[k, local], near_off[k, local]
-                lower = dot32(
-                    jnp.where(live, off_ref[q, k], zero), jnp.where(live, across, zero)
-                ).astype(jnp.bfloat16)
-                lowers.append(lower)
+                faced = off_ref[local, MIRROR[k]] if k in INSIDE else near_off[k, local]
                 facing.append(jnp.where(live, faced, zero))
-                if q < capacity:
-                    part_ref[q, k] = jnp.where(level_ref[q] == 0, part_ref[q, k], lower)
-                else:
-                    part_ref[q, k] = lower
+            lowers = lower_blocks(q, group)
             schur = dot32(jnp.concatenate(lowers, axis=1), jnp.concatenate(facing, axis=0))
             rest_ref[q - start] = before(q) - schur
 
@@ -174,61 +189,56 @@
     for side in ALONG:
         @pl.when(exists[side])
         def _():
-            for kind in range(2):
-                incoming(kind, side).wait_recv()
+            incoming(1, side).wait_recv()
+    for q in range(start, rows):
+        for j, lower in enumerate(lower_blocks(q, ALONG)):
+            lower_ref[q - start, j] = lower
+    for side in ALONG:
+        @pl.when(exists[side])
+        def _():
+            incoming(0, side).wait_recv()
+            incoming(2, side).wait_recv()
     for side in range(REMOTE):
         @pl.when(exists[side])
         def _():
-            for kind in range(2):
+            for kind in range(3 if side in ALONG else 2):
                 outgoing(kind, side).wait_send()
 
 
 def finish(
-    capacity, named_ref, level_ref, inv_ref, part_ref, rest_ref, mine_ref, far_off, far_inv,
-    pivot_hbm, factor_hbm, pivot_ref, lower_ref, sems,
+    capacity, named_ref, level_ref, inv_ref, part_ref, rest_ref, lower_ref, far_off, pivot_hbm, factor_hbm, pivot_ref, sems
 ):
     rows, slots, size, _ = part_ref.shape
     start = rows - capacity
     zero = jnp.zeros((size, size), jnp.bfloat16)
-    late = pl.ds(start, capacity)
     soon = pl.ds(0, start)
     stores = [
         pltpu.make_async_copy(source, target, sems.at[i])
         for i, (source, target) in enumerate([
-            (part_ref.at[soon], factor_hbm.at[soon]),
-            (part_ref.at[late, pl.ds(SIDEWAYS[0], 2)], factor_hbm.at[late, pl.ds(SIDEWAYS[0], 2)]),
-            (part_ref.at[late, pl.ds(INSIDE[0], 2)], factor_hbm.at[late, pl.ds(INSIDE[0], 2)]),
+            (part_ref, factor_hbm),
             (inv_ref.at[soon], pivot_hbm.at[soon]),
-            (lower_ref, factor_hbm.at[late, pl.ds(ALONG[0], 2)]),
-            (pivot_ref, pivot_hbm.at[late]),
+            (pivot_ref, pivot_hbm.at[pl.ds(start, capacity)]),
         ])
     ]
-    for store in stores[:4]:
-        store.start()
+    stores[0].start()
+    stores[1].start()
     pick = picker(named_ref, rows, capacity)
     pivots = []
     for q in range(start, rows):
-        lowers, facing = [], []
+        facing = []
         for j, k in enumerate(ALONG):
             live, local = pick(q, k)
-            lower = dot32(
-                jnp.where(live, mine_ref[q - start, j], zero), jnp.where(live, far_inv[j, local], zero)
-            ).astype(jnp.bfloat16)
-            lowers.append(lower)
             facing.append(jnp.where(live, far_off[j, local], zero))
-            if q < capacity:
-                lower = jnp.where(level_ref[q] == 0, part_ref[q, k], lower)
-            lower_ref[q - start, j] = lower
+        lowers = [lower_ref[q - start, j] for j in range(len(ALONG))]
         schur = dot32(jnp.concatenate(lowers, axis=1), jnp.concatenate(facing, axis=0))
         pivots.append(rest_ref[q - start] - schur)
-    stores[4].start()
     second = inverses(pivots, False)
     for q in range(start, rows):
         value = second[q - start]
         if q < capacity:
             value = jnp.where(level_ref[q] == 0, inv_ref[q], value)
         pivot_ref[q - start] = value
-    stores[5].start()
+    stores[2].start()
     for store in stores:
         store.wait()
 
@@ -259,20 +269,20 @@
                 shape(capacity, dtype=jnp.float32),
                 shape(capacity, 2),
                 shape(2, capacity),
-                shape(2, capacity),
             ),
             in_specs=[hbm] * 4,
-            out_specs=(vmem,) * 6,
+            out_specs=(vmem,) * 5,
             scratch_shapes=[
+                room(2, capacity),
                 room(rows),
                 room(rows, slots),
                 pltpu.SMEM(neighbors.shape, jnp.int32),
                 pltpu.SMEM(levels.shape, jnp.int32),
                 room(2, capacity),
                 room(2, capacity),
-                pltpu.SemaphoreType.DMA((5,)),
-                pltpu.SemaphoreType.DMA((2, REMOTE)),
-                pltpu.SemaphoreType.DMA((2, REMOTE)),
+                pltpu.SemaphoreType.DMA((4,)),
+                pltpu.SemaphoreType.DMA((3, REMOTE)),
+                pltpu.SemaphoreType.DMA((3, REMOTE)),
             ],
             compiler_params=pltpu.CompilerParams(
                 collective_id=0, has_side_effects=True, vmem_limit_bytes=VMEM_LIMIT
@@ -282,9 +292,9 @@
             lambda *refs: finish(capacity, *refs),
             name="finish",
             out_shape=(shape(rows), shape(rows, slots)),
-            in_specs=[smem] * 2 + [vmem] * 6,
+            in_specs=[smem] * 2 + [vmem] * 5,
             out_specs=(hbm, hbm),
-            scratch_shapes=[room(capacity), room(capacity, 2), pltpu.SemaphoreType.DMA((6,))],
+            scratch_shapes=[room(capacity), pltpu.SemaphoreType.DMA((3,))],
             compiler_params=pltpu.CompilerParams(vmem_limit_bytes=VMEM_LIMIT),
         )(neighbors, levels, *carried)
 

time: 21.2 us -> 20.8 us (0.981)
  Pallas kernels: 20.3 us -> 20 us
    pallas_call x1, Pallas kernels: 3.64 us -> 3.07 us  [shards(): pl.pallas_call(lambda *refs: finish(capacity, *refs), name='finish', out_...]
    pallas_call x1, Pallas kernels: 16.7 us -> 16.9 us  [shards(): pl.pallas_call(lambda *refs: exchange(sizes, capacity, *refs), name='exch...]
where the time goes in v3:
time: 20.8 us; the launch traced here: 20.7 us
  Pallas kernels  20 us (96%)
  between operations  0.67 us (3%)
    pallas_call x1, Pallas kernels, shards(): pl.pallas_call(lambda *refs: exchange(sizes, capacity, *refs), name='exch...  16.9 us
    pallas_call x1, Pallas kernels, shards(): pl.pallas_call(lambda *refs: finish(capacity, *refs), name='finish', out_...  3.07 us

profile of v3, /device:TPU:1, one launch (start us, length us, event | category | flops | bytes accessed | tf_op | source)
XLA Modules:
  0.0 20.7 jit_solution(1829202243302403407)
XLA Ops:
  0.6 0.0 copy-start.1
  0.6 0.0 copy-start
  0.7 16.9 %exchange.1 = (bf16[6,128,128]{2,1,0:T(8,128)(2,1)S(1)}, bf16[8,6,128,128]{3,2,1,0:T(8,128)(2,1)S(1)}, f32[6,128,128]{2,1,0:T(8,128)S(1)}, bf16[6,2,128,128]{3,2...) custom-call(bf16[8,128,128]{2,1,0:T(8,128)(2,1)} %refs_0_.2, bf16[8,6,128,128]{3,2,1,0:T(8,128)(2,1)} %refs_1_.2, ...), custom_call_target="tpu_custom_call" | custom-call | tf_op jit(solution)/shard_map/exchange/pallas_call | solution.py:263
  17.6 0.0 copy-done.1
  17.6 0.0 copy-done
  17.6 3.1 %finish.1 = (bf16[8,128,128]{2,1,0:T(8,128)(2,1)}, bf16[8,6,128,128]{3,2,1,0:T(8,128)(2,1)}) custom-call(s32[8,6]{1,0:T(8,128)S(1)} %copy-done, s32[8]{0:T(128)S(1)} %copy-done.1, bf16[6,128,128]{2,1,0:T(8,128)(2,1)S(1)} %get-tuple-element.7.refs_2_, bf16[8,6,128,128]{3,2,1,0:T(8,128)(2,1)S(1)} %get-tuple-element.8.refs_3_, ...), custom_call_target="tpu_custom_call" | custom-call | tf_op jit(solution)/shard_map/finish/pallas_call | solution.py:291
Async XLA Ops:
  0.6 17.0 %copy-start.1 = (s32[8]{0:T(128)S(1)}, s32[8]{0:T(128)}, u32[]{:S(2)}) copy-start(s32[8]{0:T(128)} %refs_1_.3) | copy-start | bytes 100
  0.6 17.0 %copy-start = (s32[8,6]{1,0:T(8,128)S(1)}, s32[8,6]{1,0:T(8,128)}, u32[]{:S(2)}) copy-start(s32[8,6]{1,0:T(8,128)} %refs_0_.3) | copy-start | bytes 580

commit v4 on v3

--- a/solution.py
+++ b/solution.py
@@ -63,8 +63,8 @@
 
 def exchange(
     sizes, capacity, diag_hbm, off_hbm, named_hbm, level_hbm,
-    inv_ref, part_ref, rest_ref, lower_ref, far_off,
-    far_inv, diag_ref, off_ref, named_ref, level_ref, near_off, near_inv, local_sem, send_sem, recv_sem,
+    pivot_ref, part_ref,
+    inv_ref, rest_ref, lower_ref, far_off, far_inv, diag_ref, off_ref, named_ref, level_ref, near_off, near_inv, local_sem, send_sem, recv_sem,
 ):
     rows, slots, size, _ = off_ref.shape
     start = rows - capacity
@@ -198,31 +198,6 @@
         def _():
             incoming(0, side).wait_recv()
             incoming(2, side).wait_recv()
-    for side in range(REMOTE):
-        @pl.when(exists[side])
-        def _():
-            for kind in range(3 if side in ALONG else 2):
-                outgoing(kind, side).wait_send()
-
-
-def finish(
-    capacity, named_ref, level_ref, inv_ref, part_ref, rest_ref, lower_ref, far_off, pivot_hbm, factor_hbm, pivot_ref, sems
-):
-    rows, slots, size, _ = part_ref.shape
-    start = rows - capacity
-    zero = jnp.zeros((size, size), jnp.bfloat16)
-    soon = pl.ds(0, start)
-    stores = [
-        pltpu.make_async_copy(source, target, sems.at[i])
-        for i, (source, target) in enumerate([
-            (part_ref, factor_hbm),
-            (inv_ref.at[soon], pivot_hbm.at[soon]),
-            (pivot_ref, pivot_hbm.at[pl.ds(start, capacity)]),
-        ])
-    ]
-    stores[0].start()
-    stores[1].start()
-    pick = picker(named_ref, rows, capacity)
     pivots = []
     for q in range(start, rows):
         facing = []
@@ -233,14 +208,30 @@
         schur = dot32(jnp.concatenate(lowers, axis=1), jnp.concatenate(facing, axis=0))
         pivots.append(rest_ref[q - start] - schur)
     second = inverses(pivots, False)
-    for q in range(start, rows):
-        value = second[q - start]
-        if q < capacity:
-            value = jnp.where(level_ref[q] == 0, inv_ref[q], value)
-        pivot_ref[q - start] = value
-    stores[2].start()
-    for store in stores:
-        store.wait()
+    for i in range(rows):
+        if i < start:
+            value = inv_ref[i]
+        elif i < capacity:
+            value = jnp.where(level_ref[i] == 0, inv_ref[i], second[i - start])
+        else:
+            value = second[i - start]
+        pivot_ref[i] = value
+    for side in range(REMOTE):
+        @pl.when(exists[side])
+        def _():
+            for kind in range(3 if side in ALONG else 2):
+                outgoing(kind, side).wait_send()
+
+
+def store(pivot_ref, part_ref, pivot_hbm, factor_hbm, sems):
+    rows = part_ref.shape[0]
+    copies = [
+        pltpu.make_async_copy(part_ref.at[i], factor_hbm.at[i], sems.at[i]) for i in range(rows)
+    ] + [pltpu.make_async_copy(pivot_ref, pivot_hbm, sems.at[rows])]
+    for copy in copies:
+        copy.start()
+    for copy in copies:
+        copy.wait()
 
 
 def solution(mesh):
@@ -252,10 +243,9 @@
         block = (size, size)
         hbm = pl.BlockSpec(memory_space=pltpu.HBM)
         vmem = pl.BlockSpec(memory_space=pltpu.VMEM)
-        smem = pl.BlockSpec(memory_space=pltpu.SMEM)
-
-        def shape(*lead, dtype=jnp.bfloat16):
-            return jax.ShapeDtypeStruct(lead + block, dtype)
+
+        def shape(*lead):
+            return jax.ShapeDtypeStruct(lead + block, jnp.bfloat16)
 
         def room(*lead):
             return pltpu.VMEM(lead + block, jnp.bfloat16)
@@ -263,16 +253,14 @@
         carried = pl.pallas_call(
             lambda *refs: exchange(sizes, capacity, *refs),
             name="exchange",
-            out_shape=(
-                shape(capacity),
-                shape(rows, slots),
-                shape(capacity, dtype=jnp.float32),
-                shape(capacity, 2),
-                shape(2, capacity),
-            ),
+            out_shape=(shape(rows), shape(rows, slots)),
             in_specs=[hbm] * 4,
-            out_specs=(vmem,) * 5,
+            out_specs=(vmem, vmem),
             scratch_shapes=[
+                room(capacity),
+                pltpu.VMEM((capacity,) + block, jnp.float32),
+                room(capacity, 2),
+                room(2, capacity),
                 room(2, capacity),
                 room(rows),
                 room(rows, slots),
@@ -289,14 +277,14 @@
             ),
         )(*[pltpu.with_memory_space_constraint(x, pltpu.HBM) for x in (diag_blocks, off_blocks, neighbors, levels)])
         return pl.pallas_call(
-            lambda *refs: finish(capacity, *refs),
-            name="finish",
+            store,
+            name="store",
             out_shape=(shape(rows), shape(rows, slots)),
-            in_specs=[smem] * 2 + [vmem] * 5,
+            in_specs=[vmem] * 2,
             out_specs=(hbm, hbm),
-            scratch_shapes=[room(capacity), pltpu.SemaphoreType.DMA((3,))],
+            scratch_shapes=[pltpu.SemaphoreType.DMA((rows + 1,))],
             compiler_params=pltpu.CompilerParams(vmem_limit_bytes=VMEM_LIMIT),
-        )(neighbors, levels, *carried)
+        )(*carried)
 
     blocks = P(("row", "col"), None, None)
     wide = P(("row", "col"), None, None, None)

time: 20.8 us -> 20.3 us (0.976)
  the two profiles are of different devices: /device:TPU:1 before, /device:TPU:33 now
where the time goes in v4:
time: 20.3 us; the launch traced here: 20.2 us
  Pallas kernels  19.5 us (96%)
  between operations  0.64 us (3%)
    pallas_call x1, Pallas kernels, shards(): pl.pallas_call(lambda *refs: exchange(sizes, capacity, *refs), name='exch...  18.2 us
    pallas_call x1, Pallas kernels, shards(): pl.pallas_call(store, name='store', out_shape=(shape(rows), shape(rows, s...  1.3 us

profile of v4, /device:TPU:33, one launch (start us, length us, event | category | flops | bytes accessed | tf_op | source)
XLA Modules:
  0.0 20.2 jit_solution(10224366695962305402)
XLA Ops:
  0.6 18.2 %exchange.1 = (bf16[8,128,128]{2,1,0:T(8,128)(2,1)S(1)}, bf16[8,6,128,128]{3,2,1,0:T(8,128)(2,1)S(1)}) custom-call(bf16[8,128,128]{2,1,0:T(8,128)(2,1)} %refs_0_.1, bf16[8,6,128,128]{3,2,1,0:T(8,128)(2,1)} %refs_1_.1, s32[8,6]{1,0:T(8,128)} %refs_2_.1, s32[8]{0:T(128)} %refs_3_.1), custom_call_target="tpu_custom_call" | custom-call | tf_op jit(solution)/shard_map/exchange/pallas_call | solution.py:253
  18.9 1.3 %store.1 = (bf16[8,128,128]{2,1,0:T(8,128)(2,1)}, bf16[8,6,128,128]{3,2,1,0:T(8,128)(2,1)}) custom-call(bf16[8,128,128]{2,1,0:T(8,128)(2,1)S(1)} %get-tuple-element.4.pivot_ref, bf16[8,6,128,128]{3,2,1,0:T(8,128)(2,1)S(1)} %get-tuple-element.5.part_ref), custom_call_target="tpu_custom_call" | custom-call | tf_op jit(solution)/shard_map/store/pallas_call | solution.py:279

commit v5 on v4

--- a/solution.py
+++ b/solution.py
@@ -64,7 +64,7 @@
 def exchange(
     sizes, capacity, diag_hbm, off_hbm, named_hbm, level_hbm,
     pivot_ref, part_ref,
-    inv_ref, rest_ref, lower_ref, far_off, far_inv, diag_ref, off_ref, named_ref, level_ref, near_off, near_inv, local_sem, send_sem, recv_sem,
+    inv_ref, rest_ref, lower_ref, far_off, far_inv, diag_ref, off_ref, named_ref, level_ref, near_off, near_inv, local_sem, send_sem, recv_sem, answer,
 ):
     rows, slots, size, _ = off_ref.shape
     start = rows - capacity
@@ -78,8 +78,10 @@
         exists.append((target[axis] < sizes[axis]) if move[axis] > 0 else (target[axis] >= 0))
 
     barrier = pltpu.get_barrier_semaphore()
+    odd = lax.rem(here[0], 2) == 1
+    even = jnp.logical_not(odd)
     for side in range(REMOTE):
-        @pl.when(exists[side])
+        @pl.when(exists[side] if side in ALONG else jnp.logical_and(exists[side], odd))
         def _():
             pl.semaphore_signal(barrier, inc=1, device_id=there[side], device_id_type=MESH)
     loads = [
@@ -93,7 +95,10 @@
     ]
     for load in loads:
         load.start()
-    pl.semaphore_wait(barrier, sum(flag.astype(jnp.int32) for flag in exists))
+    pl.semaphore_wait(barrier, sum(
+        (exists[side] if side in ALONG else jnp.logical_and(exists[side], even)).astype(jnp.int32)
+        for side in range(REMOTE)
+    ))
 
     pieces = (pl.ds(0, capacity - 1), pl.ds(0, capacity), pl.ds(capacity - 1, 1))
 
@@ -124,21 +129,37 @@
     def incoming(kind, side):
         return transfer(kind, landing(kind, side), side, side)
 
-    for side in ALONG + SIDEWAYS:
-        @pl.when(exists[side])
-        def _():
+    for side in ALONG:
+        @pl.when(exists[side])
+        def _():
+            outgoing(0, side).start()
+    for side in SIDEWAYS:
+        @pl.when(jnp.logical_and(exists[side], even))
+        def _():
+            pl.semaphore_signal(
+                answer.at[MIRROR[side]], inc=1, device_id=there[side], device_id_type=MESH
+            )
             outgoing(0, side).start()
 
     loads[0].wait()
     found = inverses([diag_ref[i].astype(jnp.float32) for i in range(capacity)], True)
     for i in range(capacity):
         inv_ref[i] = found[i]
-    for side in ALONG + SIDEWAYS:
+    for side in ALONG:
         @pl.when(exists[side])
         def _():
             outgoing(1, side).start()
-            if side in ALONG:
-                outgoing(2, side).start()
+            outgoing(2, side).start()
+    for side in SIDEWAYS:
+        @pl.when(jnp.logical_and(exists[side], even))
+        def _():
+            outgoing(1, side).start()
+
+        @pl.when(jnp.logical_and(exists[side], odd))
+        def _():
+            pl.semaphore_wait(answer.at[side], 1)
+            outgoing(0, side).start()
+            outgoing(1, side).start()
 
     for load in loads[1:]:
         load.wait()
@@ -271,6 +292,7 @@
                 pltpu.SemaphoreType.DMA((4,)),
                 pltpu.SemaphoreType.DMA((3, REMOTE)),
                 pltpu.SemaphoreType.DMA((3, REMOTE)),
+                pltpu.SemaphoreType.REGULAR((len(SIDEWAYS),)),
             ],
             compiler_params=pltpu.CompilerParams(
                 collective_id=0, has_side_effects=True, vmem_limit_bytes=VMEM_LIMIT

time: 20.3 us -> 18.9 us (0.931)
  the two profiles are of different devices: /device:TPU:33 before, /device:TPU:206 now
where the time goes in v5:
time: 18.9 us; the launch traced here: 18.8 us
  Pallas kernels  18.2 us (96%)
  between operations  0.64 us (3%)
    pallas_call x1, Pallas kernels, shards(): pl.pallas_call(lambda *refs: exchange(sizes, capacity, *refs), name='exch...  16.9 us
    pallas_call x1, Pallas kernels, shards(): pl.pallas_call(store, name='store', out_shape=(shape(rows), shape(rows, s...  1.3 us

profile of v5, /device:TPU:206, one launch (start us, length us, event | category | flops | bytes accessed | tf_op | source)
XLA Modules:
  0.0 18.8 jit_solution(14102449107500471929)
XLA Ops:
  0.6 16.9 %exchange.1 = (bf16[8,128,128]{2,1,0:T(8,128)(2,1)S(1)}, bf16[8,6,128,128]{3,2,1,0:T(8,128)(2,1)S(1)}) custom-call(bf16[8,128,128]{2,1,0:T(8,128)(2,1)} %refs_0_.1, bf16[8,6,128,128]{3,2,1,0:T(8,128)(2,1)} %refs_1_.1, s32[8,6]{1,0:T(8,128)} %refs_2_.1, s32[8]{0:T(128)} %refs_3_.1), custom_call_target="tpu_custom_call" | custom-call | tf_op jit(solution)/shard_map/exchange/pallas_call | solution.py:274
  17.5 1.3 %store.1 = (bf16[8,128,128]{2,1,0:T(8,128)(2,1)}, bf16[8,6,128,128]{3,2,1,0:T(8,128)(2,1)}) custom-call(bf16[8,128,128]{2,1,0:T(8,128)(2,1)S(1)} %get-tuple-element.4.pivot_ref, bf16[8,6,128,128]{3,2,1,0:T(8,128)(2,1)S(1)} %get-tuple-element.5.part_ref), custom_call_target="tpu_custom_call" | custom-call | tf_op jit(solution)/shard_map/store/pallas_call | solution.py:301

commit v6 on v5

--- a/solution.py
+++ b/solution.py
@@ -141,6 +141,11 @@
             )
             outgoing(0, side).start()
 
+        @pl.when(jnp.logical_and(exists[side], odd))
+        def _():
+            pl.semaphore_wait(answer.at[side], 1)
+            outgoing(0, side).start()
+
     loads[0].wait()
     found = inverses([diag_ref[i].astype(jnp.float32) for i in range(capacity)], True)
     for i in range(capacity):
@@ -151,14 +156,8 @@
             outgoing(1, side).start()
             outgoing(2, side).start()
     for side in SIDEWAYS:
-        @pl.when(jnp.logical_and(exists[side], even))
-        def _():
-            outgoing(1, side).start()
-
-        @pl.when(jnp.logical_and(exists[side], odd))
-        def _():
-            pl.semaphore_wait(answer.at[side], 1)
-            outgoing(0, side).start()
+        @pl.when(exists[side])
+        def _():
             outgoing(1, side).start()
 
     for load in loads[1:]:

time: 18.9 us -> 21.3 us (1.13)
  the two profiles are of different devices: /device:TPU:206 before, /device:TPU:1 now
where the time goes in v6:
time: 21.3 us; the launch traced here: 21.2 us
  Pallas kernels  20.5 us (96%)
  between operations  0.64 us (3%)
    pallas_call x1, Pallas kernels, shards(): pl.pallas_call(lambda *refs: exchange(sizes, capacity, *refs), name='exch...  19.2 us
    pallas_call x1, Pallas kernels, shards(): pl.pallas_call(store, name='store', out_shape=(shape(rows), shape(rows, s...  1.3 us

profile of v6, /device:TPU:1, one launch (start us, length us, event | category | flops | bytes accessed | tf_op | source)
XLA Modules:
  0.0 21.2 jit_solution(6713764456916221343)
XLA Ops:
  0.6 19.2 %exchange.1 = (bf16[8,128,128]{2,1,0:T(8,128)(2,1)S(1)}, bf16[8,6,128,128]{3,2,1,0:T(8,128)(2,1)S(1)}) custom-call(bf16[8,128,128]{2,1,0:T(8,128)(2,1)} %refs_0_.1, bf16[8,6,128,128]{3,2,1,0:T(8,128)(2,1)} %refs_1_.1, s32[8,6]{1,0:T(8,128)} %refs_2_.1, s32[8]{0:T(128)} %refs_3_.1), custom_call_target="tpu_custom_call" | custom-call | tf_op jit(solution)/shard_map/exchange/pallas_call | solution.py:273
  19.9 1.3 %store.1 = (bf16[8,128,128]{2,1,0:T(8,128)(2,1)}, bf16[8,6,128,128]{3,2,1,0:T(8,128)(2,1)}) custom-call(bf16[8,128,128]{2,1,0:T(8,128)(2,1)S(1)} %get-tuple-element.4.pivot_ref, bf16[8,6,128,128]{3,2,1,0:T(8,128)(2,1)S(1)} %get-tuple-element.5.part_ref), custom_call_target="tpu_custom_call" | custom-call | tf_op jit(solution)/shard_map/store/pallas_call | solution.py:300

commit v7 on v5

--- a/solution.py
+++ b/solution.py
@@ -20,12 +20,7 @@
     return jnp.dot(left, right, preferred_element_type=jnp.float32)
 
 
-def split(value):
-    high = value.astype(jnp.bfloat16)
-    return high, (value - high.astype(jnp.float32)).astype(jnp.bfloat16)
-
-
-def inverses(matrices, paired):
+def inverses(matrices):
     size = matrices[0].shape[0]
     row_id = lax.broadcasted_iota(jnp.int32, (size, size), 0)
     col_id = lax.broadcasted_iota(jnp.int32, (size, size), 1)
@@ -37,18 +32,10 @@
         row_norm = jnp.max(jnp.sum(magnitude, axis=1, keepdims=True), axis=0, keepdims=True)
         iterates.append(matrix.T * (1.0 / (column_norm * row_norm)))
     lefts = [matrix.astype(jnp.bfloat16) for matrix in matrices]
-    if paired:
-        lefts = [jnp.concatenate([left, left], axis=1) for left in lefts]
     for _ in range(NS_STEPS):
-        halves = [split(iterate) if paired else (iterate.astype(jnp.bfloat16),) for iterate in iterates]
-        rests = [
-            (identity - dot32(left, jnp.concatenate(half, axis=0))).astype(jnp.bfloat16)
-            for left, half in zip(lefts, halves)
-        ]
-        iterates = [
-            iterate + dot32(jnp.concatenate(half, axis=1), jnp.concatenate([rest] * len(half), axis=0))
-            for iterate, half, rest in zip(iterates, halves, rests)
-        ]
+        rounded = [iterate.astype(jnp.bfloat16) for iterate in iterates]
+        rests = [(identity - dot32(left, x)).astype(jnp.bfloat16) for left, x in zip(lefts, rounded)]
+        iterates = [iterate + dot32(x, rest) for iterate, x, rest in zip(iterates, rounded, rests)]
     return [iterate.astype(jnp.bfloat16) for iterate in iterates]
 
 
@@ -142,7 +129,7 @@
             outgoing(0, side).start()
 
     loads[0].wait()
-    found = inverses([diag_ref[i].astype(jnp.float32) for i in range(capacity)], True)
+    found = inverses([diag_ref[i].astype(jnp.float32) for i in range(capacity)])
     for i in range(capacity):
         inv_ref[i] = found[i]
     for side in ALONG:
@@ -228,7 +215,7 @@
         lowers = [lower_ref[q - start, j] for j in range(len(ALONG))]
         schur = dot32(jnp.concatenate(lowers, axis=1), jnp.concatenate(facing, axis=0))
         pivots.append(rest_ref[q - start] - schur)
-    second = inverses(pivots, False)
+    second = inverses(pivots)
     for i in range(rows):
         if i < start:
             value = inv_ref[i]

time: 18.9 us -> 18.9 us (level)
  the two profiles are of different devices: /device:TPU:206 before, /device:TPU:218 now
where the time goes in v7:
time: 18.9 us; the launch traced here: 18.8 us
  Pallas kernels  18.2 us (96%)
  between operations  0.64 us (3%)
    pallas_call x1, Pallas kernels, shards(): pl.pallas_call(lambda *refs: exchange(sizes, capacity, *refs), name='exch...  16.9 us
    pallas_call x1, Pallas kernels, shards(): pl.pallas_call(store, name='store', out_shape=(shape(rows), shape(rows, s...  1.3 us

profile of v7, /device:TPU:218, one launch (start us, length us, event | category | flops | bytes accessed | tf_op | source)
XLA Modules:
  0.0 18.8 jit_solution(12380997668834574878)
XLA Ops:
  0.6 16.9 %exchange.1 = (bf16[8,128,128]{2,1,0:T(8,128)(2,1)S(1)}, bf16[8,6,128,128]{3,2,1,0:T(8,128)(2,1)S(1)}) custom-call(bf16[8,128,128]{2,1,0:T(8,128)(2,1)} %refs_0_.1, bf16[8,6,128,128]{3,2,1,0:T(8,128)(2,1)} %refs_1_.1, s32[8,6]{1,0:T(8,128)} %refs_2_.1, s32[8]{0:T(128)} %refs_3_.1), custom_call_target="tpu_custom_call" | custom-call | tf_op jit(solution)/shard_map/exchange/pallas_call | solution.py:261
  17.5 1.3 %store.1 = (bf16[8,128,128]{2,1,0:T(8,128)(2,1)}, bf16[8,6,128,128]{3,2,1,0:T(8,128)(2,1)}) custom-call(bf16[8,128,128]{2,1,0:T(8,128)(2,1)S(1)} %get-tuple-element.4.pivot_ref, bf16[8,6,128,128]{3,2,1,0:T(8,128)(2,1)S(1)} %get-tuple-element.5.part_ref), custom_call_target="tpu_custom_call" | custom-call | tf_op jit(solution)/shard_map/store/pallas_call | solution.py:288

commit v8 on v7

--- a/solution.py
+++ b/solution.py
@@ -80,8 +80,7 @@
             (level_hbm, level_ref),
         ])
     ]
-    for load in loads:
-        load.start()
+    loads[0].start()
     pl.semaphore_wait(barrier, sum(
         (exists[side] if side in ALONG else jnp.logical_and(exists[side], even)).astype(jnp.int32)
         for side in range(REMOTE)
@@ -128,6 +127,8 @@
             )
             outgoing(0, side).start()
 
+    for load in loads[1:]:
+        load.start()
     loads[0].wait()
     found = inverses([diag_ref[i].astype(jnp.float32) for i in range(capacity)])
     for i in range(capacity):

time: 18.9 us -> 18.9 us (level)
  no operation moved by 1% of the time
where the time goes in v8:
time: 18.9 us; the launch traced here: 18.8 us
  Pallas kernels  18.2 us (96%)
  between operations  0.64 us (3%)
    pallas_call x1, Pallas kernels, shards(): pl.pallas_call(lambda *refs: exchange(sizes, capacity, *refs), name='exch...  16.9 us
    pallas_call x1, Pallas kernels, shards(): pl.pallas_call(store, name='store', out_shape=(shape(rows), shape(rows, s...  1.3 us

profile of v8, /device:TPU:218, one launch (start us, length us, event | category | flops | bytes accessed | tf_op | source)
XLA Modules:
  0.0 18.8 jit_solution(12129044958384855913)
XLA Ops:
  0.6 16.9 %exchange.1 = (bf16[8,128,128]{2,1,0:T(8,128)(2,1)S(1)}, bf16[8,6,128,128]{3,2,1,0:T(8,128)(2,1)S(1)}) custom-call(bf16[8,128,128]{2,1,0:T(8,128)(2,1)} %refs_0_.1, bf16[8,6,128,128]{3,2,1,0:T(8,128)(2,1)} %refs_1_.1, s32[8,6]{1,0:T(8,128)} %refs_2_.1, s32[8]{0:T(128)} %refs_3_.1), custom_call_target="tpu_custom_call" | custom-call | tf_op jit(solution)/shard_map/exchange/pallas_call | solution.py:262
  17.5 1.3 %store.1 = (bf16[8,128,128]{2,1,0:T(8,128)(2,1)}, bf16[8,6,128,128]{3,2,1,0:T(8,128)(2,1)}) custom-call(bf16[8,128,128]{2,1,0:T(8,128)(2,1)S(1)} %get-tuple-element.4.pivot_ref, bf16[8,6,128,128]{3,2,1,0:T(8,128)(2,1)S(1)} %get-tuple-element.5.part_ref), custom_call_target="tpu_custom_call" | custom-call | tf_op jit(solution)/shard_map/store/pallas_call | solution.py:289
